TPU v7x, 32 devices: a whole 2x2x4 slice. The times are simulated.
32 devices in a mesh: gx: 4 (over x, core), gy: 8 (over z, y).
Axes of the slice: x: 2, y: 2, z: 4, core: 2. Of those that a mesh axis runs over, the one named last changes fastest.
Arguments:
- fields: float32 [4, 64, 128, 128], P(None, 'gx', 'gy'), may hold values from -6 to 6
- lift: float32 [32, 4], replicated, may hold values from -3 to 3
- lift_bias: float32 [32], replicated, may hold values from -3 to 3
- spectral_in: float32 [256, 2, 8, 32, 64], P(('gx', 'gy')), may hold values from -0.03125 to 0.03125
- bypass_in: float32 [64, 32], replicated, may hold values from -1 to 1
- bias_in: float32 [64], replicated, may hold values from -3 to 3
- spectral_out: float32 [256, 2, 8, 64, 32], P(('gx', 'gy')), may hold values from -0.046875 to 0.046875
- bypass_out: float32 [32, 64], replicated, may hold values from -0.75 to 0.75
- bias_out: float32 [32], replicated, may hold values from -3 to 3
- project: float32 [4, 32], replicated, may hold values from -1 to 1
- project_bias: float32 [4], replicated, may hold values from -3 to 3
Outputs:
- result: float32 [4, 64, 128, 128], P(None, 'gx', 'gy')
All inputs are finite; a program needn't handle non-finite values.
Results may differ from a plain program's by a relative error of at most 0.000058.
Values sent between devices are 32-bit elements; how exact they have to be, the bound alone decides.
A program may use at most 64 MiB of HBM per device.

v0:
```python
import math

import jax
import jax.numpy as jnp
from jax import lax
from jax.sharding import PartitionSpec as P

KX = 16
KY = 16
KZ = 8


def product(formula, left, right):
    return jnp.einsum(formula, left, right, precision=lax.Precision.HIGHEST)


def tables(places, length, count, centered):
    frequency = jnp.arange(count, dtype=jnp.int32)
    if centered:
        frequency = jnp.where(frequency < count // 2, frequency, frequency - count)
    turns = places[:, None] * frequency[None, :] % length
    angle = turns.astype(jnp.float32) * (2.0 * math.pi / length)
    return (jnp.cos(angle), jnp.sin(angle))


def forward(field, x_places, y_places, x_length, y_length, scale):
    z_length = field.shape[3]
    z_cos, z_sin = tables(jnp.arange(z_length, dtype=jnp.int32), z_length, KZ, False)
    real_part = product("cxyz,zk->cxyk", field, z_cos)
    imag_part = -product("cxyz,zk->cxyk", field, z_sin)
    y_cos, y_sin = tables(y_places, y_length, KY, True)
    real_next = product("cxyk,yj->cxjk", real_part, y_cos) + product(
        "cxyk,yj->cxjk", imag_part, y_sin
    )
    imag_next = product("cxyk,yj->cxjk", imag_part, y_cos) - product(
        "cxyk,yj->cxjk", real_part, y_sin
    )
    x_cos, x_sin = tables(x_places, x_length, KX, True)
    real_last = product("cxjk,xi->ijkc", real_next, x_cos) + product(
        "cxjk,xi->ijkc", imag_next, x_sin
    )
    imag_last = product("cxjk,xi->ijkc", imag_next, x_cos) - product(
        "cxjk,xi->ijkc", real_next, x_sin
    )
    stacked = jnp.stack([real_last, imag_last], axis=2)
    return stacked.reshape((KX * KY, 2, KZ, stacked.shape[4])) * scale


def mix_modes(spectrum, weights):
    real_in = spectrum[:, 0]
    imag_in = spectrum[:, 1]
    real_weight = weights[:, 0]
    imag_weight = weights[:, 1]
    real_out = product("mkc,mkcd->mkd", real_in, real_weight) - product(
        "mkc,mkcd->mkd", imag_in, imag_weight
    )
    imag_out = product("mkc,mkcd->mkd", real_in, imag_weight) + product(
        "mkc,mkcd->mkd", imag_in, real_weight
    )
    return jnp.stack([real_out, imag_out], axis=1)


def inverse(spectrum, x_places, y_places, x_length, y_length, z_length, scale):
    grid = spectrum.reshape((KX, KY, 2, KZ, spectrum.shape[3]))
    real_part = grid[:, :, 0]
    imag_part = grid[:, :, 1]
    x_cos, x_sin = tables(x_places, x_length, KX, True)
    real_next = product("ijkc,xi->xjkc", real_part, x_cos) - product(
        "ijkc,xi->xjkc", imag_part, x_sin
    )
    imag_next = product("ijkc,xi->xjkc", real_part, x_sin) + product(
        "ijkc,xi->xjkc", imag_part, x_cos
    )
    y_cos, y_sin = tables(y_places, y_length, KY, True)
    real_last = product("xjkc,yj->xykc", real_next, y_cos) - product(
        "xjkc,yj->xykc", imag_next, y_sin
    )
    imag_last = product("xjkc,yj->xykc", real_next, y_sin) + product(
        "xjkc,yj->xykc", imag_next, y_cos
    )
    z_cos, z_sin = tables(jnp.arange(z_length, dtype=jnp.int32), z_length, KZ, False)
    return (
        product("xykc,zk->cxyz", real_last, z_cos) - product("xykc,zk->cxyz", imag_last, z_sin)
    ) * scale


def modes_mixed(partial_value, weights):
    rows = partial_value.shape[0]
    flat = partial_value.reshape((rows, -1))
    totals = lax.psum(flat, ("gx", "gy"))
    owned_rows = weights.shape[0]
    owner_index = lax.axis_index("gx") * lax.axis_size("gy") + lax.axis_index("gy")
    summed = lax.dynamic_slice_in_dim(totals, owner_index * owned_rows, owned_rows, 0)
    owned = mix_modes(summed.reshape((-1,) + partial_value.shape[1:]), weights)
    owned_flat = owned.reshape((owned.shape[0], -1))
    whole = lax.all_gather(
        lax.all_gather(owned_flat, "gy", axis=0, tiled=True), "gx", axis=0, tiled=True
    )
    return whole.reshape((rows, 2, KZ, -1))


def on_device(
    fields,
    lift,
    lift_bias,
    spectral_in,
    bypass_in,
    bias_in,
    spectral_out,
    bypass_out,
    bias_out,
    project,
    project_bias,
):
    x_cells = fields.shape[1]
    y_cells = fields.shape[2]
    z_cells = fields.shape[3]
    channels = lift.shape[0]
    x_length = x_cells * lax.axis_size("gx")
    y_length = y_cells * lax.axis_size("gy")
    x_first = lax.axis_index("gx") * x_cells
    y_first = lax.axis_index("gy") * y_cells
    local_x = x_first + jnp.arange(x_cells, dtype=jnp.int32)
    local_y = y_first + jnp.arange(y_cells, dtype=jnp.int32)
    coarse_x = x_first // 2 + jnp.arange(x_cells // 2, dtype=jnp.int32)
    coarse_y = y_first // 2 + jnp.arange(y_cells // 2, dtype=jnp.int32)
    back = math.sqrt(2.0 / (KX * KY * KZ))
    lifted = product("dc,cxyz->dxyz", lift, fields) + lift_bias[:, None, None, None]
    spectrum = forward(
        lifted, local_x, local_y, x_length, y_length, 1.0 / math.sqrt(x_length * y_length * z_cells)
    )
    mixed = modes_mixed(spectrum, spectral_in)
    pooled = lifted.reshape((channels, x_cells // 2, 2, y_cells // 2, 2, z_cells)).mean(axis=(2, 4))
    coarse = jax.nn.gelu(
        inverse(mixed, 2 * coarse_x, 2 * coarse_y, x_length, y_length, z_cells, back)
        + product("ec,cxyz->exyz", bypass_in, pooled)
        + bias_in[:, None, None, None],
        approximate=False,
    )
    spectrum = forward(
        coarse,
        coarse_x,
        coarse_y,
        x_length // 2,
        y_length // 2,
        1.0 / math.sqrt(x_length * y_length * z_cells / 4.0),
    )
    mixed = modes_mixed(spectrum, spectral_out)
    narrow = product("dc,cxyz->dxyz", bypass_out, coarse)
    widened = jnp.repeat(jnp.repeat(narrow, 2, axis=1), 2, axis=2)
    fine = jax.nn.gelu(
        inverse(mixed, local_x, local_y, x_length, y_length, z_cells, back)
        + widened
        + bias_out[:, None, None, None],
        approximate=False,
    )
    return product("oc,cxyz->oxyz", project, fine + lifted) + project_bias[:, None, None, None]


def solution(mesh):
    in_specs = (
        P(None, "gx", "gy", None),
        P(),
        P(),
        P(("gx", "gy"), None, None, None, None),
        P(),
        P(),
        P(("gx", "gy"), None, None, None, None),
        P(),
        P(),
        P(),
        P(),
    )
    out_specs = P(None, "gx", "gy", None)
    return jax.shard_map(
        on_device, mesh=mesh, in_specs=in_specs, out_specs=out_specs, check_vma=False
    )
```

profile of v0, /device:TPU:0, one launch (start us, length us, event | category | flops | bytes accessed | tf_op | source)
XLA Modules:
  0.0 527.8 jit_solution(12517158401896493713)
XLA Ops:
  7.6 5.2 convolution_add_fusion
  12.8 16.3 %convolution_negate_fusion = f32[32,16,16,8]{0,3,2,1:T(8,128)S(1)} fusion(f32[32,16,16,128]{3,0,2,1:T(8,128)S(1)} %convolution_add_fusion), kind=kOutput, calls=%fused_computation.135 | convolution fusion | flops 100743168 | bytes 4456448 | tf_op jit(solution)/shard_map/cxyz,zk->cxyk/dot_general | solution.py:14
  29.1 16.5 %fusion.260 = f32[32,16,16,8]{0,3,2,1:T(8,128)S(1)} fusion(f32[32,16,16,128]{3,0,2,1:T(8,128)S(1)} %convolution_add_fusion), kind=kOutput, calls=%fused_computation.340 | convolution fusion | flops 100677632 | bytes 4456448 | tf_op jit(solution)/shard_map/cxyz,zk->cxyk/dot_general | solution.py:14
  50.3 1.8 fusion.156
  52.1 2.0 fusion.160
  54.1 1.8 fusion.106
  55.8 1.8 fusion.107
  62.2 131.9 %all-reduce.3.cloned.1.call-done = f32[256,512]{0,1:T(8,128)} async-done(((f32[256,512]{0,1:T(8,128)}), f32[256,512]{0,1:T(8,128)}) %all-reduce.3.cloned.1.call-update) | async-done | bytes 524304 | tf_op jit(solution)/shard_map/psum | solution.py:90
  199.4 32.7 %all_gather.12 = f32[64,1024]{1,0:T(8,128)} all-gather(f32[8,1024]{1,0:T(8,128)S(1)} %reshape.74), channel_id=1, replica_groups=mesh['gx'=4,'gy'=8] {'gy'}, dimensions={0}, use_global_device_ids=true | all-gather | bytes 294912 | tf_op jit(solution)/shard_map/all_gather | solution.py:97
  232.2 3.8 reduce_sum.9
  236.0 12.0 %all-gather.2.cloned.1.call-done = f32[256,1024]{1,0:T(8,128)} async-done(((f32[64,1024]{1,0:T(8,128)}), f32[256,1024]{1,0:T(8,128)}) %all-gather.2.cloned.1.call-update) | async-done | bytes 1048592 | tf_op jit(solution)/shard_map/all_gather | solution.py:96
  248.0 2.1 reshape_reshape.6
  258.2 3.5 fusion.187
  261.7 3.6 fusion.189
  265.3 6.4 %fusion.63 = f32[64,8,8,128]{3,0,2,1:T(8,128)S(1)} fusion(f32[128,8,8,64]{0,3,2,1:T(8,128)S(1)} %fusion.189, f32[128,8,8,64]{0,3,2,1:T(8,128)S(1)} %fusion.187, f32[64]{0:T(128)S(1)} %copy-done.11, f32[32,8,8,128]{3,0,2,1:T(8,128)S(1)} %copy-done.7, f32[64,32]{0,1:T(8,128)S(1)} %copy-done.9), kind=kOutput, calls=%fused_computation.70 | convolution fusion | flops 237240320 | bytes 7348480 | tf_op jit(solution)/shard_map/ec,cxyz->exyz/dot_general | solution.py:14
  271.8 5.0 convolution_negate_fusion.1
  276.7 5.4 %fusion.257 = f32[64,8,8,8]{0,3,2,1:T(8,128)S(1)} fusion(f32[64,8,8,128]{3,0,2,1:T(8,128)S(1)} %fusion.63), kind=kOutput, calls=%fused_computation.337 | convolution fusion | flops 50345984 | bytes 2228224 | tf_op jit(solution)/shard_map/cxyz,zk->cxyk/dot_general | solution.py:14
  286.4 2.3 fusion.179
  292.9 2.5 fusion.111
  299.4 2.2 convolution_bitcast_fusion
  301.6 128.5 %all-reduce.5.cloned.1.call-done = f32[256,1024]{0,1:T(8,128)} async-done(((f32[256,1024]{0,1:T(8,128)}), f32[256,1024]{0,1:T(8,128)}) %all-reduce.5.cloned.1.call-update) | async-done | bytes 1048592 | tf_op jit(solution)/shard_map/psum | solution.py:90
  431.6 1.9 fusion.122
  433.5 1.8 fusion.128
  435.4 1.8 fusion.126
  437.1 1.8 fusion.124
  439.0 30.5 %all_gather.14 = f32[64,512]{1,0:T(8,128)S(1)} all-gather(f32[8,512]{1,0:T(8,128)S(1)} %reshape.77), channel_id=1, replica_groups=mesh['gx'=4,'gy'=8] {'gy'}, dimensions={0}, use_global_device_ids=true | all-gather | bytes 147456 | tf_op jit(solution)/shard_map/all_gather | solution.py:97
  469.5 7.2 %all_gather.15 = f32[256,512]{1,0:T(8,128)S(1)} all-gather(f32[64,512]{1,0:T(8,128)S(1)} %all_gather.14), channel_id=1, replica_groups=mesh['gx'=4,'gy'=8] {'gx'}, dimensions={0}, use_global_device_ids=true | all-gather | bytes 655360 | tf_op jit(solution)/shard_map/all_gather | solution.py:96
  482.2 1.7 fusion.152
  487.3 2.1 fusion.105
  491.1 6.8 %fusion.138 = f32[128,16,16,32]{0,3,2,1:T(8,128)S(1)} fusion(f32[16,16,8,32]{3,1,2,0:T(8,128)S(1)} %fusion.104), kind=kOutput, calls=%fused_computation.174 | convolution fusion | flops 100677632 | bytes 4456448 | tf_op jit(solution)/shard_map/xykc,zk->cxyz/dot_general | solution.py:14
  497.9 6.9 %fusion.140 = f32[128,16,16,32]{0,3,2,1:T(8,128)S(1)} fusion(f32[16,16,8,32]{3,1,2,0:T(8,128)S(1)} %fusion.105), kind=kOutput, calls=%fused_computation.176 | convolution fusion | flops 100677632 | bytes 4456448 | tf_op jit(solution)/shard_map/xykc,zk->cxyz/dot_general | solution.py:14
  507.3 12.9 %fusion.117 = f32[4,16,16,128]{3,0,2,1:T(4,128)S(1)} fusion(f32[32,16,16,128]{3,0,2,1:T(8,128)S(1)} %copy-done.3, f32[32,16,16,128]{3,0,2,1:T(8,128)S(1)} %bitcast.301, f32[128,16,16,32]{0,3,2,1:T(8,128)S(1)} %fusion.140, f32[128,16,16,32]{0,3,2,1:T(8,128)S(1)} %fusion.138, f32[32]{0:T(128)S(1)} %copy-done.12, f32[4]{0:T(128)S(1)} %copy-done.13, ...), kind=kOutput, calls=%fused_computation.147 | convolution fusion | flops 122814464 | bytes 17302160 | tf_op jit(solution)/shard_map/oc,cxyz->oxyz/dot_general | solution.py:14
  (99 shorter events, 51.5 us)
Async XLA Ops:
  6.5 1.0 copy-start
  6.5 187.6 %all-reduce.3.cloned.1.call-start = ((), (), s32[]{:S(2)}) async-start(), calls=%async_computation | async-start | bytes 1048576 | tf_op jit(solution)/shard_map/psum | solution.py:90
  12.7 16.3 %copy-start.2 = (f32[32,16,16,128]{3,0,2,1:T(8,128)}, f32[32,16,16,128]{3,0,2,1:T(8,128)S(1)}, u32[]{:S(2)}) copy-start(f32[32,16,16,128]{3,0,2,1:T(8,128)S(1)} %convolution_add_fusion) | copy-start | bytes 12582916
  59.6 135.7 %copy-start.4 = (f32[8,2,8,32,64]{4,3,2,1,0:T(8,128)S(1)}, f32[8,2,8,32,64]{4,3,2,1,0:T(8,128)}, u32[]{:S(2)}) copy-start(f32[8,2,8,32,64]{4,3,2,1,0:T(8,128)} %param.14) | copy-start | bytes 3145732
  62.2 185.8 %all-gather.2.cloned.1.call-start = ((), (), s32[]{:S(2)}) async-start(), calls=%async_computation.1 | async-start | bytes 1310720 | tf_op jit(solution)/shard_map/all_gather | solution.py:96
  232.1 198.0 %all-reduce.5.cloned.1.call-start = ((), (), s32[]{:S(2)}) async-start(), calls=%async_computation.2 | async-start | bytes 2097152 | tf_op jit(solution)/shard_map/psum | solution.py:90
  258.1 7.1 %copy-start.7 = (f32[32,8,8,128]{3,0,2,1:T(8,128)S(1)}, f32[32,8,8,128]{3,0,2,1:T(8,128)}, u32[]{:S(2)}) copy-start(f32[32,8,8,128]{3,0,2,1:T(8,128)} %reduce_sum.9) | copy-start | bytes 3145732
  258.2 7.1 %copy-start.9 = (f32[64,32]{0,1:T(8,128)S(1)}, f32[64,32]{0,1:T(8,128)}, u32[]{:S(2)}) copy-start(f32[64,32]{0,1:T(8,128)} %param.15) | copy-start | bytes 24580
  258.2 7.1 %copy-start.11 = (f32[64]{0:T(128)S(1)}, f32[64]{0:T(128)}, u32[]{:S(2)}) copy-start(f32[64]{0:T(128)} %param.16) | copy-start | bytes 772
  296.7 2.7 copy-start.8
  301.6 129.9 %copy-start.5 = (f32[8,2,8,64,32]{3,4,2,1,0:T(8,128)S(1)}, f32[8,2,8,64,32]{3,4,2,1,0:T(8,128)}, u32[]{:S(2)}) copy-start(f32[8,2,8,64,32]{3,4,2,1,0:T(8,128)} %param.17) | copy-start | bytes 3145732
  497.9 6.9 %copy-start.6 = (f32[32,8,8,128]{3,0,2,1:T(8,128)S(1)}, f32[32,8,8,128]{3,0,2,1:T(8,128)}, u32[]{:S(2)}) copy-start(f32[32,8,8,128]{3,0,2,1:T(8,128)} %convolution_bitcast_fusion) | copy-start | bytes 3145732
  505.1 2.2 copy-start.3
  505.1 2.2 copy-start.10
  505.1 2.2 copy-start.12
  505.1 2.2 copy-start.13
  507.3 13.7 %copy-start.1 = (f32[4,16,16,128]{3,2,1,0:T(8,128)S(1)}, f32[4,16,16,128]{3,2,1,0:T(8,128)}, u32[]{:S(2)}) copy-start(f32[4,16,16,128]{3,2,1,0:T(8,128)} %param.11) | copy-start | bytes 1572868
Sparse Core Ops, SparseCore 0:
  62.3 131.7 all-reduce.2
  232.2 15.6 all-gather.1
  299.5 130.6 all-reduce.4
where the time goes:
time: 537 us; the launch traced here: 528 us
  waiting for transfers between devices  272 us (51%)
  matrix products  145 us (27%)
  blocking collectives  70.4 us (13%)
  local copies, waits for them, and re-layouts  19.8 us (4%)
  between operations  13.9 us (3%)
  other arithmetic  5.76 us (1%)
    psum x2, waiting for transfers between devices, modes_mixed(): totals = lax.psum(flat, ('gx', 'gy'))  260 us
    dot_general x52, matrix products, product(): return jnp.einsum(formula, left, right, precision=lax.Precision.HIGHEST)  145 us
    all_gather x2, blocking collectives, modes_mixed(): lax.all_gather(owned_flat, 'gy', axis=0, tiled=True)  63.3 us
    all_gather x1, waiting for transfers between devices, modes_mixed(): lax.all_gather(lax.all_gather(owned_flat, 'gy', axis=0, tiled=True), 'gx'...  12 us
  transfers between devices with their start and end apart: 3, of which 3 were waited for; matrix products, arithmetic and copies ran while one was open for 1% of the time, Pallas kernels for 0%

commit v1 on v0

v1 whole, which is shorter than its diff:
```python
import functools
import math

import jax
import jax.numpy as jnp
import numpy as np
from jax import lax
from jax.experimental import pallas as pl
from jax.experimental.pallas import tpu as pltpu
from jax.sharding import PartitionSpec as P

KX = 16
KY = 16
KZ = 8
YB = 8
LB = 128
F32 = jnp.float32
BF16 = jnp.bfloat16
MESH = pl.DeviceIdType.MESH


def freq(count):
    f = np.arange(count)
    return np.where(f < count // 2, f, f - count)


def halves(table):
    high = table.astype(np.float32).astype(jnp.bfloat16)
    low = (table - high.astype(np.float64)).astype(np.float32).astype(jnp.bfloat16)
    return np.stack([high, low])


def angles(places, frequency, length):
    turns = np.mod(places[:, None] * frequency[None, :], length)
    return turns * (2.0 * math.pi / length)


def z_table(z_length):
    ang = angles(np.arange(z_length), np.arange(KZ), z_length)
    table = np.zeros((YB, z_length, 2, YB, KZ))
    for y in range(YB):
        table[y, :, 0, y] = np.cos(ang)
        table[y, :, 1, y] = -np.sin(ang)
    return table.reshape(YB * z_length, LB)


def y_table(blocks, cells, length, groups):
    per = KY // groups
    frequency = freq(KY)
    out = np.zeros((blocks, cells // YB, 2, YB, KZ, groups, LB))
    for b in range(blocks):
        ang = angles(b * cells + np.arange(cells), frequency, length)
        for y in range(cells):
            for j in range(KY):
                c, s = np.cos(ang[y, j]), np.sin(ang[y, j])
                for k in range(KZ):
                    re = (j % per) * KZ + k
                    im = per * KZ + re
                    at = (b, y // YB)
                    out[at + (0, y % YB, k, j // per, re)] = c
                    out[at + (1, y % YB, k, j // per, re)] = s
                    out[at + (0, y % YB, k, j // per, im)] = -s
                    out[at + (1, y % YB, k, j // per, im)] = c
    return out.reshape(blocks, cells // YB * LB, groups * LB)


def x_angles(blocks, cells, length):
    return angles(np.arange(blocks * cells), freq(KX), length).reshape(blocks, cells, KX)


def split(value):
    high = value.astype(BF16)
    return high, (value - high.astype(F32)).astype(BF16)


def mul(a, b):
    return jnp.dot(a, b, preferred_element_type=F32)


def mul3(a, b):
    return mul(a[0], b[0]) + (mul(a[1], b[0]) + mul(a[0], b[1]))


def gelu(v):
    return (0.5 * v) * (1.0 + lax.erf(v * math.sqrt(0.5)))


def kernel(
    A, B, cells_x, scale1, scale2, gain,
    f_ref, pk_ref, fk_ref, lift_ref, lbias_ref, bp_ref, wo_ref, bo_ref, pr_ref, pl_ref,
    tzf_ref, tzi_ref, cs_ref, w1_hbm, w2_hbm, tx_hbm, yf1_hbm, yfc_hbm, yic_hbm, yi2_hbm,
    o_ref,
    w1, w2, tx, yf1, yfc, yic, yi2,
    buf1, r1, mx, mt1, ag1, yb1, ya1, zc, fx2, r2, buf2, r3, mt2, ag2, yb2, ya2, nar, yr1, yr2,
    csem, ssem, rsem,
):
    a = lax.axis_index("gx")
    b = lax.axis_index("gy")
    me = a * B + b
    IL = KX // A
    H = B // IL
    J = KY // H
    N = A * B
    C1 = lift_ref.shape[0]
    C2 = wo_ref.shape[2]
    CIN = lift_ref.shape[1]
    hx = cells_x // 2

    loads = [
        pltpu.make_async_copy(tx_hbm.at[a], tx, csem.at[0]),
        pltpu.make_async_copy(yf1_hbm.at[b], yf1, csem.at[1]),
        pltpu.make_async_copy(w1_hbm, w1, csem.at[2]),
        pltpu.make_async_copy(yic_hbm.at[b], yic, csem.at[3]),
        pltpu.make_async_copy(yfc_hbm.at[b], yfc, csem.at[4]),
        pltpu.make_async_copy(w2_hbm, w2, csem.at[5]),
        pltpu.make_async_copy(yi2_hbm.at[b], yi2, csem.at[6]),
    ]
    for load in loads:
        load.start()

    barrier = pltpu.get_barrier_semaphore()
    for step in range(1, N):
        peer = lax.rem(me + step, N)
        pl.semaphore_signal(
            barrier, inc=1, device_id=(peer // B, lax.rem(peer, B)), device_id_type=MESH
        )

    lane = lax.broadcasted_iota(jnp.int32, (1, LB), 1)
    sign_f = jnp.where(lane < LB // 2, 1.0, -1.0).astype(F32)

    def rot_f(v):
        return pltpu.roll(v, LB // 2, 1) * sign_f

    def rot_i(v):
        return pltpu.roll(v, LB // 2, 1) * -sign_f

    tzf = (tzf_ref[0], tzf_ref[1])
    width = tzf_ref.shape[1]
    zs = []
    for ch in range(2):
        zs.append(mul3(split(f_ref[:, ch * width:(ch + 1) * width]), tzf))
    loads[0].wait()
    us = []
    for z in zs:
        us.append(mul3((tx[0], tx[1]), split(jnp.concatenate([z, rot_f(z)], axis=0))))
    loads[1].wait()
    part = mul3(split(jnp.concatenate(us, axis=1)), (yf1[0], yf1[1]))
    for i in range(KX):
        for h in range(H):
            buf1[i * H + h] = part[i * CIN:(i + 1) * CIN, h * LB:(h + 1) * LB]
    r1[me] = buf1[me]
    pl.semaphore_wait(barrier, N - 1)

    sends = []
    phase = []
    for step in range(1, N):
        peer = lax.rem(me + step, N)
        phase.append(pltpu.make_async_remote_copy(
            src_ref=buf1.at[peer], dst_ref=r1.at[me], send_sem=ssem.at[peer], recv_sem=rsem.at[me],
            device_id=(peer // B, lax.rem(peer, B)), device_id_type=MESH,
        ))
    for copy in phase:
        copy.start()
    sends += phase
    loads[2].wait()
    for step in range(1, N):
        peer = lax.rem(me + step, N)
        pltpu.make_async_remote_copy(
            src_ref=buf1.at[peer], dst_ref=r1.at[peer], send_sem=ssem.at[peer], recv_sem=rsem.at[peer],
            device_id=(peer // B, lax.rem(peer, B)), device_id_type=MESH,
        ).wait_recv()

    first_slot = {1: N, 2: N + B, 3: N + B + A, 4: N + B + 2 * A, 5: N + 2 * B + 2 * A, 6: N + 3 * B + 2 * A}

    def spread(source, target, axis, count, mine, slot):
        copies = []
        arrivals = []
        base = first_slot[slot]
        for step in range(1, count):
            peer = lax.rem(mine + step, count)
            where = (peer, b) if axis == "gx" else (a, peer)
            for index, group in ((mine, copies), (peer, arrivals)):
                group.append(pltpu.make_async_remote_copy(
                    src_ref=source(peer), dst_ref=target.at[index],
                    send_sem=ssem.at[base + peer], recv_sem=rsem.at[base + index],
                    device_id=where, device_id_type=MESH,
                ))
        for copy in copies:
            copy.start()
        sends.extend(copies)
        return arrivals

    def arrive(copies):
        for copy in copies:
            copy.wait_recv()

    def mix(st, w, width_out):
        mx[...] = jnp.zeros_like(mx)
        for j in range(J):
            for k in range(KZ):
                q = j * KZ + k
                p = J * KZ + q
                re = st[:, q:q + 1]
                im = st[:, p:p + 1]
                wr = w[j, 0, k]
                wi = w[j, 1, k]
                mx[q:q + 1, :width_out] = jnp.sum(re * wr - im * wi, axis=0, keepdims=True)
                mx[p:p + 1, :width_out] = jnp.sum(re * wi + im * wr, axis=0, keepdims=True)
        return mx[...].T[:width_out]

    s4 = jnp.sum(r1[...], axis=0) * scale1
    st = lift_ref[:, 0:1] * s4[0:1]
    for c in range(1, CIN):
        st = st + lift_ref[:, c:c + 1] * s4[c:c + 1]
    first = jnp.where((lane == 0) & (me == 0), gain, 0.0).astype(F32)
    st = st + lbias_ref[...] * first
    mixed = mix(st, w1, C2)
    mt1[...] = mixed
    ag1[b] = mixed
    copies = spread(lambda peer: mt1, ag1, "gy", B, b, 1)
    loads[3].wait()
    arrive(copies)

    def y_back(ag, table):
        rows = [jnp.concatenate([ag[i * H + h] for i in range(IL)], axis=0) for h in range(H)]
        return mul3(split(jnp.concatenate(rows, axis=1)), (table[0], table[1]))

    y = y_back(ag1, yic).reshape(IL, C2, LB)
    yb1[...] = y
    ya1[a] = y
    arrive(spread(lambda peer: yb1, ya1, "gx", A, a, 2))
    for i in range(KX):
        yr1[i] = rot_i(ya1[i // IL, i % IL])

    HC = hx * KX

    def coarse_step(x, carry):
        acc = jnp.zeros((C2, LB), F32)
        for i in range(KX):
            c = cs_ref[a, x * KX + i]
            s = cs_ref[a, HC + x * KX + i]
            acc = acc + (c * ya1[i // IL, i % IL] + s * yr1[i])
        v = mul3(split(acc), (tzi_ref[0], tzi_ref[1])) + mul(bp_ref[...], pk_ref[x])
        g = split(gelu(v))
        nar[x] = mul3((wo_ref[0], wo_ref[1]), g)
        zc[x] = mul3(g, (tzf_ref[0], tzf_ref[1]))
        return carry

    lax.fori_loop(0, hx, coarse_step, 0)

    def x_step(i, carry):
        re = jnp.zeros((C2, LB), F32)
        im = jnp.zeros((C2, LB), F32)
        for x in range(hx):
            re = re + cs_ref[a, x * KX + i] * zc[x]
            im = im + cs_ref[a, HC + x * KX + i] * zc[x]
        fx2[i // IL, i % IL] = re + rot_f(im)
        return carry

    lax.fori_loop(0, KX, x_step, 0)
    copies = spread(lambda peer: fx2.at[peer], r2, "gx", A, a, 3)
    r2[a] = fx2[a]
    loads[4].wait()
    arrive(copies)
    total = jnp.sum(r2[...], axis=0).reshape(IL * C2, LB)
    out = mul3(split(total), (yfc[0], yfc[1]))
    for i in range(IL):
        for h in range(H):
            buf2[i * H + h] = out[i * C2:(i + 1) * C2, h * LB:(h + 1) * LB]
    copies = spread(lambda peer: buf2.at[peer], r3, "gy", B, b, 4)
    r3[b] = buf2[b]
    loads[5].wait()
    arrive(copies)
    st = jnp.sum(r3[...], axis=0) * scale2
    mixed = mix(st, w2, C1)
    mt2[...] = mixed
    ag2[b] = mixed
    copies = spread(lambda peer: mt2, ag2, "gy", B, b, 5)
    loads[6].wait()
    arrive(copies)
    y = y_back(ag2, yi2).reshape(IL, C1, 2 * LB)
    yb2[...] = y
    ya2[a] = y
    arrive(spread(lambda peer: yb2, ya2, "gx", A, a, 6))
    for i in range(KX):
        for ch in range(2):
            part = slice(ch * LB, (ch + 1) * LB)
            yr2[i, :, part] = rot_i(ya2[i // IL, i % IL, :, part])

    FC = cells_x * KX
    zn = width // YB

    def fine_step(x, carry):
        acc = jnp.zeros((C1, 2 * LB), F32)
        for i in range(KX):
            c = cs_ref[a, 2 * HC + x * KX + i]
            s = cs_ref[a, 2 * HC + FC + x * KX + i]
            acc = acc + (c * ya2[i // IL, i % IL] + s * yr2[i])
        for ch in range(2):
            v = mul3(split(acc[:, ch * LB:(ch + 1) * LB]), (tzi_ref[0], tzi_ref[1]))
            pieces = []
            for yy in range(YB):
                at = (ch * YB + yy) // 2 * zn
                pieces.append(nar[x // 2, :, at:at + zn])
            v = v + jnp.concatenate(pieces, axis=1) + bo_ref[...]
            g = split(gelu(v))
            cols = slice(ch * width, (ch + 1) * width)
            o_ref[x, :, cols] = mul3((pr_ref[0], pr_ref[1]), g) + mul(pl_ref[...], fk_ref[x, :, cols])
        return carry

    lax.fori_loop(0, cells_x, fine_step, 0)
    for copy in sends:
        copy.wait_send()


def rough(value):
    return lax.reduce_precision(value, 8, 7)


def hi_lo(value):
    high = rough(value)
    return jnp.stack([high.astype(BF16), rough(value - high).astype(BF16)])


def left16(matrix, bias):
    high = rough(matrix)
    low = rough(matrix - high)
    b0 = rough(bias)
    b1 = rough(bias - b0)
    b2 = rough(bias - b0 - b1)
    zero = jnp.zeros((matrix.shape[0], 1), F32)
    return jnp.concatenate(
        [high, high, low, b0[:, None], b1[:, None], b2[:, None], zero], axis=1
    ).astype(BF16)


def right16(value):
    high = rough(value)
    low = rough(value - high)
    ones = jnp.ones((value.shape[0], 4, value.shape[2]), F32)
    return jnp.concatenate([high, low, high, ones], axis=1).astype(BF16)


def product(left, right):
    return jnp.dot(left, right, precision=lax.Precision.HIGHEST)


def on_device(
    A, B, fields, lift, lift_bias, spectral_in, bypass_in, bias_in, spectral_out, bypass_out,
    bias_out, proj, proj_bias,
):
    cin, xc, yc, zc = fields.shape
    C1 = lift.shape[0]
    C2 = bypass_in.shape[0]
    NX = xc * A
    NY = yc * B
    IL = KX // A
    H = B // IL
    J = KY // H
    N = A * B
    width = YB * zc
    cells = float(NX * NY * zc)
    back = math.sqrt(2.0 / (KX * KY * KZ))

    tz = z_table(zc)
    tzf = halves(tz)
    tzi = halves(np.ascontiguousarray(tz.T) * back)
    fine_x = x_angles(A, xc, NX)
    half_x = x_angles(A, xc // 2, NX // 2)
    eye = np.eye(cin)
    tx = np.stack([
        np.concatenate([np.kron(np.cos(fine_x[i].T), eye), np.kron(np.sin(fine_x[i].T), eye)], axis=1)
        for i in range(A)
    ])
    cs = np.concatenate([
        np.cos(half_x).reshape(A, -1), np.sin(half_x).reshape(A, -1),
        np.cos(fine_x).reshape(A, -1), np.sin(fine_x).reshape(A, -1),
    ], axis=1).astype(np.float32)
    yf1 = y_table(B, yc, NY, H)
    yfc = y_table(B, yc // 2, NY // 2, H)

    def per_device(table):
        return jnp.asarray(np.ascontiguousarray(np.swapaxes(halves(table), 0, 1)))

    tx_t = per_device(tx)
    yf1_t = per_device(yf1)
    yfc_t = per_device(yfc)
    yic_t = per_device(np.swapaxes(yfc, 1, 2))
    yi2_t = per_device(np.swapaxes(yf1, 1, 2))

    rows = jnp.transpose(fields, (1, 0, 2, 3)).reshape(xc, cin, yc * zc)
    pooled = fields.reshape(cin, xc // 2, 2, yc // 2, 2, zc).mean(axis=(2, 4))
    pooled = jnp.transpose(pooled, (1, 0, 2, 3)).reshape(xc // 2, cin, width)
    bp = left16(product(bypass_in, lift), product(bypass_in, lift_bias) + bias_in)
    pj = left16(product(proj, lift), product(proj, lift_bias) + proj_bias)

    vmem = pl.BlockSpec(memory_space=pltpu.VMEM)
    anywhere = pl.BlockSpec(memory_space=pl.ANY)
    V = pltpu.VMEM
    out = pl.pallas_call(
        functools.partial(
            kernel, A, B, xc, 1.0 / math.sqrt(cells), 1.0 / math.sqrt(cells / 4.0), math.sqrt(cells)
        ),
        out_shape=jax.ShapeDtypeStruct((xc, cin, yc * zc), F32),
        in_specs=[vmem] * 12 + [pl.BlockSpec(memory_space=pltpu.SMEM)] + [anywhere] * 7,
        out_specs=vmem,
        scratch_shapes=[
            V(spectral_in.shape, F32), V(spectral_out.shape, F32),
            V(tx_t.shape[1:], BF16), V(yf1_t.shape[1:], BF16), V(yfc_t.shape[1:], BF16),
            V(yic_t.shape[1:], BF16), V(yi2_t.shape[1:], BF16),
            V((N, cin, LB), F32), V((N, cin, LB), F32), V((LB, LB), F32),
            V((C2, LB), F32), V((B, C2, LB), F32),
            V((IL, C2, LB), F32), V((A, IL, C2, LB), F32),
            V((xc // 2, C2, LB), F32), V((A, IL, C2, LB), F32), V((A, IL, C2, LB), F32),
            V((B, C2, LB), F32), V((B, C2, LB), F32),
            V((C1, LB), F32), V((B, C1, LB), F32),
            V((IL, C1, 2 * LB), F32), V((A, IL, C1, 2 * LB), F32),
            V((xc // 2, C1, width), F32), V((KX, C2, LB), F32), V((KX, C1, 2 * LB), F32),
            pltpu.SemaphoreType.DMA((7,)),
            pltpu.SemaphoreType.DMA((N + 3 * B + 3 * A,)), pltpu.SemaphoreType.DMA((N + 3 * B + 3 * A,)),
        ],
        compiler_params=pltpu.CompilerParams(
            collective_id=0, has_side_effects=True, vmem_limit_bytes=60 * 1024 * 1024
        ),
    )(
        rows.reshape(xc * cin, yc * zc), right16(pooled), right16(rows), lift, lift_bias[:, None], bp,
        hi_lo(bypass_out), bias_out[:, None], hi_lo(proj), pj, jnp.asarray(tzf), jnp.asarray(tzi),
        jnp.asarray(cs), spectral_in, spectral_out, tx_t, yf1_t, yfc_t, yic_t, yi2_t,
    )
    return jnp.transpose(out.reshape(xc, cin, yc, zc), (1, 0, 2, 3))


def solution(mesh):
    A = mesh.shape["gx"]
    B = mesh.shape["gy"]
    in_specs = (
        P(None, "gx", "gy", None), P(), P(), P(("gx", "gy"), None, None, None, None), P(), P(),
        P(("gx", "gy"), None, None, None, None), P(), P(), P(), P(),
    )
    return jax.shard_map(
        functools.partial(on_device, A, B), mesh=mesh, in_specs=in_specs,
        out_specs=P(None, "gx", "gy", None), check_vma=False,
    )
```

time: 537 us -> 99 us (0.18); the launches traced: 528 us -> 97.6 us
  waiting for transfers between devices: 272 us -> 0 us
  matrix products: 145 us -> 3.3 us
  Pallas kernels: 0 us -> 74.9 us
  blocking collectives: 70.4 us -> 0 us
  between operations: 13.9 us -> 0.09 us
  local copies, waits for them, and re-layouts: 19.8 us -> 12.5 us
    psum x2 -> x0, waiting for transfers between devices: 260 us -> none  [modes_mixed(): totals = lax.psum(flat, ('gx', 'gy'))]
    dot_general x52 -> x4, matrix products: 145 us -> 3.3 us  [product(): return jnp.dot(left, right, precision=lax.Precision.HIGHEST)]
    pallas_call x0 -> x1, Pallas kernels: none -> 74.9 us  [on_device(): pl.pallas_call(functools.partial(kernel, A, B, xc, 1.0 / math.sqrt(cells)...]
    all_gather x3 -> x0, blocking collectives: 70.4 us -> none  [the longest x2 63.3 us: modes_mixed(): lax.all_gather(owned_flat, 'gy', axis=0, tiled=True)]
    all_gather x1 -> x0, waiting for transfers between devices: 12 us -> none  [modes_mixed(): lax.all_gather(lax.all_gather(owned_flat, 'gy', axis=0, tiled=True), 'gx'...]
    another operation x6 -> x1, local copies, waits for them, and re-layouts: 7.77 us -> 0.01 us  [the longest x4 5.14 us: forward(): stacked = jnp.stack([real_last, imag_last], axis=2)]
  transfers between devices with their start and end apart: 3 -> 0, of which waited for: 3 -> 0; matrix products, arithmetic and copies ran while one was open for 1% -> 0% of each run, Pallas kernels for 0% -> 0%
where the time goes in v1:
time: 99 us; the launch traced here: 97.6 us
  Pallas kernels  74.9 us (76%)
  local copies, waits for them, and re-layouts  12.5 us (13%)
  other arithmetic  6.86 us (7%)
  matrix products  3.3 us (3%)
    pallas_call x1, Pallas kernels, on_device(): pl.pallas_call(functools.partial(kernel, A, B, xc, 1.0 / math.sqrt(cells)...  74.9 us
    unnamed x9, local copies, waits for them, and re-layouts  5.68 us
    dot_general x4, matrix products, product(): return jnp.dot(left, right, precision=lax.Precision.HIGHEST)  3.3 us
    another operation x4, other arithmetic, hi_lo(): return jnp.stack([high.astype(BF16), rough(value - high).astype(BF16)])  2.62 us
    concatenate x2, other arithmetic, right16(): return jnp.concatenate([high, low, high, ones], axis=1).astype(BF16)  2.3 us
    reshape x2, local copies, waits for them, and re-layouts, on_device(): return jnp.transpose(out.reshape(xc, cin, yc, zc), (1, 0, 2, 3))  2.15 us

profile of v1, /device:TPU:0, one launch (start us, length us, event | category | flops | bytes accessed | tf_op | source)
XLA Modules:
  0.0 97.6 jit_solution(15771829671698621862)
XLA Ops:
  0.0 0.0 copy-start
  0.0 0.1 pad.11.clone
  0.1 0.6 copy-done
  0.7 0.8 fusion.22
  1.5 0.8 fusion.27
  2.4 0.1 copy.40
  2.5 0.1 copy.39
  2.6 0.1 copy.38
  2.7 0.8 fusion.11
  3.5 0.1 concatenate.18
  3.6 0.8 fusion.15
  4.4 0.7 concatenate.19.pl_ref
  5.1 0.7 fusion.17
  5.8 0.6 pad_maximum_fusion.1.pr_ref
  6.4 0.7 copy.43.bp_ref
  7.1 1.3 %copy.44.bo_ref = f32[32,1]{1,0:T(8,128)} copy(f32[32,1]{0,1:T(1,128)} %bitcast.76) | data formatting | bytes 256 | tf_op jit(solution)/shard_map/broadcast_in_dim | solution.py:427
  8.4 1.3 %copy.42.lbias_ref = f32[32,1]{1,0:T(8,128)} copy(f32[32,1]{0,1:T(1,128)} %bitcast.75) | data formatting | bytes 256 | tf_op jit(solution)/shard_map/broadcast_in_dim | solution.py:426
  9.7 1.4 %copy.41.lift_ref = f32[32,4]{1,0:T(8,128)} copy(f32[32,4]{0,1:T(4,128)} %param.20) | data formatting | bytes 1024 | tf_op args[1]
  11.1 0.7 fusion.9
  11.8 0.6 pad_maximum_fusion.wo_ref
  12.4 1.4 %reduce_sum.9 = f32[4,8,8,128]{3,2,1,0:T(8,128)S(1)} reduce(f32[4,8,2,8,2,128]{5,4,3,2,1,0:T(2,128)} %bitcast.70, f32[]{:T(128)} %constant.12.clone.1), dimensions={2,4}, to_apply=%region_0.0 | reduce | flops 98304 | bytes 655364 | tf_op jit(solution)/shard_map/reduce_sum | solution.py:392
  13.9 0.1 fusion.5
  14.0 0.8 maximum_maximum_fusion.1.pk_ref
  14.8 0.1 reshape.21
  14.9 0.4 fusion.3
  15.3 0.0 copy-start.2
  15.4 1.5 %maximum_maximum_fusion.fk_ref = bf16[16,16,2048]{2,1,0:T(8,128)(2,1)} fusion(bf16[16,4,2048]{2,1,0:T(4,128)(2,1)S(1)} %get-tuple-element.6, bf16[16,4,2048]{2,1,0:T(4,128)(2,1)S(1)} %get-tuple-element.5, bf16[16]{0:T(256)(128)(2,1)S(1)} %pad.11.clone), kind=kLoop, calls=%fused_computation.4 | loop fusion | flops 4194304 | bytes 1572896 | tf_op jit(solution)/shard_map/concatenate | solution.py:341
  16.9 1.0 copy.56
  17.8 2.7 %copy.45.w2_hbm = f32[8,2,8,64,32]{4,3,2,1,0:T(8,128)} copy(f32[8,2,8,64,32]{3,4,2,1,0:T(8,128)S(1)} %copy-done.2) | data formatting | bytes 2097152 | tf_op args[6]
  20.6 74.9 %shard_map.181 = f32[16,4,2048]{2,1,0:T(4,128)} custom-call(f32[64,2048]{1,0:T(8,128)} %bitcast.73, bf16[8,16,1024]{2,1,0:T(8,128)(2,1)} %maximum_maximum_fusion.1.pk_ref, bf16[16,16,2048]{2,1,0:T(8,128)(2,1)} %maximum_maximum_fusion.fk_ref, f32[32,4]{1,0:T(8,128)} %copy.41.lift_ref, f32[32,1]{1,0:T(8,128)} %copy.42.lbias_ref, bf16[64,16]{1,0:T(8,128)(2,1)} %copy.43.bp_ref, ...), custom_call_target="tpu_custom_call" | custom-call | tf_op jit(solution)/shard_map/pallas_call | solution.py:400
  95.5 1.3 %reshape.15 = f32[16,4,16,128]{3,2,1,0:T(8,128)S(1)} reshape(f32[16,4,2048]{2,1,0:T(4,128)} %shard_map.181) | data formatting | bytes 1048576 | tf_op jit(solution)/shard_map/reshape | solution.py:430
  96.8 0.8 copy.57
  (9 shorter events, 0.1 us)
Async XLA Ops:
  0.0 0.7 copy-start
  0.0 14.8 %copy-start.1 = (f32[4,16,16,128]{3,2,1,0:T(8,128)S(1)}, f32[4,16,16,128]{3,2,1,0:T(8,128)}, u32[]{:S(2)}) copy-start(f32[4,16,16,128]{3,2,1,0:T(8,128)} %param.19) | copy-start | bytes 1572868
  15.3 2.5 %copy-start.2 = (f32[8,2,8,64,32]{3,4,2,1,0:T(8,128)S(1)}, f32[8,2,8,64,32]{3,4,2,1,0:T(8,128)}, u32[]{:S(2)}) copy-start(f32[8,2,8,64,32]{3,4,2,1,0:T(8,128)} %param.25) | copy-start | bytes 3145732

commit v2 on v1

--- a/solution.py
+++ b/solution.py
@@ -87,11 +87,11 @@
 
 def kernel(
     A, B, cells_x, scale1, scale2, gain,
-    f_ref, pk_ref, fk_ref, lift_ref, lbias_ref, bp_ref, wo_ref, bo_ref, pr_ref, pl_ref,
+    f_ref, lift_ref, lbias_ref, byp_ref, bi_ref, wo_ref, bo_ref, pr_ref, pb_ref,
     tzf_ref, tzi_ref, cs_ref, w1_hbm, w2_hbm, tx_hbm, yf1_hbm, yfc_hbm, yic_hbm, yi2_hbm,
     o_ref,
     w1, w2, tx, yf1, yfc, yic, yi2,
-    buf1, r1, mx, mt1, ag1, yb1, ya1, zc, fx2, r2, buf2, r3, mt2, ag2, yb2, ya2, nar, yr1, yr2,
+    buf1, r1, mx, mt1, ag1, yb1, ya1, zc, fx2, r2, buf2, r3, mt2, ag2, yb2, ya2, nar, yr1, yr2, pk_ref, fk_ref, t16,
     csem, ssem, rsem,
 ):
     a = lax.axis_index("gx")
@@ -101,9 +101,8 @@
     H = B // IL
     J = KY // H
     N = A * B
-    C1 = lift_ref.shape[0]
-    C2 = wo_ref.shape[2]
-    CIN = lift_ref.shape[1]
+    CIN, C1 = lift_ref.shape
+    C2 = wo_ref.shape[1]
     hx = cells_x // 2
 
     loads = [
@@ -163,6 +162,39 @@
         copy.start()
     sends += phase
     loads[2].wait()
+    mx[...] = jnp.zeros_like(mx)
+    mx[0:CIN, :C1] = lift_ref[...]
+    mx[CIN:CIN + 1, :C1] = lbias_ref[...]
+    mx[CIN + 1:CIN + 2, :C1] = bo_ref[...]
+    lift8 = jnp.concatenate([mx[0:8, :C1]], axis=0)
+    columns = mx[...].T[:C1]
+    bo_col = columns[:, CIN + 1:CIN + 2]
+
+    def left16(matrix, bias):
+        n = matrix.shape[1]
+        high, low = split(matrix[0:CIN])
+        b0 = bias.astype(BF16)
+        rest = bias - b0.astype(F32)
+        b1 = rest.astype(BF16)
+        b2 = (rest - b1.astype(F32)).astype(BF16)
+        mx[...] = jnp.zeros_like(mx)
+        mx[0:CIN, :n] = high.astype(F32)
+        mx[CIN:2 * CIN, :n] = high.astype(F32)
+        mx[2 * CIN:3 * CIN, :n] = low.astype(F32)
+        for row, value in enumerate((b0, b1, b2)):
+            mx[3 * CIN + row:3 * CIN + row + 1, :n] = value.astype(F32)
+        return mx[...].T[:n, :16].astype(BF16)
+
+    highest = lax.Precision.HIGHEST
+    m = jnp.dot(lift8, byp_ref[...], precision=highest, preferred_element_type=F32)
+    bp16 = left16(m, m[CIN:CIN + 1] + bi_ref[...])
+    m = lax.dot_general(
+        lift8, pr_ref[...], (((1,), (1,)), ((), ())), precision=highest, preferred_element_type=F32
+    )
+    pl16 = left16(m, m[CIN:CIN + 1] + pb_ref[...])
+    wo2 = split(wo_ref[...])
+    pr2 = split(pr_ref[...])
+    t16[...] = jnp.ones_like(t16)
     for step in range(1, N):
         peer = lax.rem(me + step, N)
         pltpu.make_async_remote_copy(
@@ -209,15 +241,36 @@
         return mx[...].T[:width_out]
 
     s4 = jnp.sum(r1[...], axis=0) * scale1
-    st = lift_ref[:, 0:1] * s4[0:1]
+    st = columns[:, 0:1] * s4[0:1]
     for c in range(1, CIN):
-        st = st + lift_ref[:, c:c + 1] * s4[c:c + 1]
+        st = st + columns[:, c:c + 1] * s4[c:c + 1]
     first = jnp.where((lane == 0) & (me == 0), gain, 0.0).astype(F32)
-    st = st + lbias_ref[...] * first
+    st = st + columns[:, CIN:CIN + 1] * first
     mixed = mix(st, w1, C2)
     mt1[...] = mixed
     ag1[b] = mixed
     copies = spread(lambda peer: mt1, ag1, "gy", B, b, 1)
+    zn = width // YB
+
+    def fill(value):
+        n = value.shape[1]
+        high, low = split(value)
+        t16[0:CIN, :n] = high.astype(F32)
+        t16[CIN:2 * CIN, :n] = low.astype(F32)
+        t16[2 * CIN:3 * CIN, :n] = high.astype(F32)
+        return t16[:, :n].astype(BF16)
+
+    for x in range(hx):
+        one = f_ref[2 * x * CIN:(2 * x + 1) * CIN]
+        two = f_ref[(2 * x + 1) * CIN:(2 * x + 2) * CIN]
+        fk_ref[2 * x] = fill(one)
+        fk_ref[2 * x + 1] = fill(two)
+        both = one + two
+        pieces = [
+            both[:, 2 * y * zn:(2 * y + 1) * zn] + both[:, (2 * y + 1) * zn:(2 * y + 2) * zn]
+            for y in range(YB)
+        ]
+        pk_ref[x] = fill(jnp.concatenate(pieces, axis=1) * 0.25)
     loads[3].wait()
     arrive(copies)
 
@@ -240,9 +293,9 @@
             c = cs_ref[a, x * KX + i]
             s = cs_ref[a, HC + x * KX + i]
             acc = acc + (c * ya1[i // IL, i % IL] + s * yr1[i])
-        v = mul3(split(acc), (tzi_ref[0], tzi_ref[1])) + mul(bp_ref[...], pk_ref[x])
+        v = mul3(split(acc), (tzi_ref[0], tzi_ref[1])) + mul(bp16, pk_ref[x])
         g = split(gelu(v))
-        nar[x] = mul3((wo_ref[0], wo_ref[1]), g)
+        nar[x] = mul3(wo2, g)
         zc[x] = mul3(g, (tzf_ref[0], tzf_ref[1]))
         return carry
 
@@ -271,8 +324,19 @@
     r3[b] = buf2[b]
     loads[5].wait()
     arrive(copies)
-    st = jnp.sum(r3[...], axis=0) * scale2
-    mixed = mix(st, w2, C1)
+    st = (jnp.sum(r3[...], axis=0) * scale2).T
+    mixed = jnp.zeros((C1, LB), F32)
+    for j in range(J):
+        for k in range(KZ):
+            q = j * KZ + k
+            p = J * KZ + q
+            re = st[q:q + 1]
+            im = st[p:p + 1]
+            wr = w2[j, 0, k]
+            wi = w2[j, 1, k]
+            real = jnp.sum(re * wr - im * wi, axis=1, keepdims=True)
+            imag = jnp.sum(re * wi + im * wr, axis=1, keepdims=True)
+            mixed = jnp.where(lane == q, real, jnp.where(lane == p, imag, mixed))
     mt2[...] = mixed
     ag2[b] = mixed
     copies = spread(lambda peer: mt2, ag2, "gy", B, b, 5)
@@ -288,7 +352,6 @@
             yr2[i, :, part] = rot_i(ya2[i // IL, i % IL, :, part])
 
     FC = cells_x * KX
-    zn = width // YB
 
     def fine_step(x, carry):
         acc = jnp.zeros((C1, 2 * LB), F32)
@@ -302,47 +365,15 @@
             for yy in range(YB):
                 at = (ch * YB + yy) // 2 * zn
                 pieces.append(nar[x // 2, :, at:at + zn])
-            v = v + jnp.concatenate(pieces, axis=1) + bo_ref[...]
+            v = v + jnp.concatenate(pieces, axis=1) + bo_col
             g = split(gelu(v))
             cols = slice(ch * width, (ch + 1) * width)
-            o_ref[x, :, cols] = mul3((pr_ref[0], pr_ref[1]), g) + mul(pl_ref[...], fk_ref[x, :, cols])
+            o_ref[x, :, cols] = mul3(pr2, g) + mul(pl16, fk_ref[x, :, cols])
         return carry
 
     lax.fori_loop(0, cells_x, fine_step, 0)
     for copy in sends:
         copy.wait_send()
-
-
-def rough(value):
-    return lax.reduce_precision(value, 8, 7)
-
-
-def hi_lo(value):
-    high = rough(value)
-    return jnp.stack([high.astype(BF16), rough(value - high).astype(BF16)])
-
-
-def left16(matrix, bias):
-    high = rough(matrix)
-    low = rough(matrix - high)
-    b0 = rough(bias)
-    b1 = rough(bias - b0)
-    b2 = rough(bias - b0 - b1)
-    zero = jnp.zeros((matrix.shape[0], 1), F32)
-    return jnp.concatenate(
-        [high, high, low, b0[:, None], b1[:, None], b2[:, None], zero], axis=1
-    ).astype(BF16)
-
-
-def right16(value):
-    high = rough(value)
-    low = rough(value - high)
-    ones = jnp.ones((value.shape[0], 4, value.shape[2]), F32)
-    return jnp.concatenate([high, low, high, ones], axis=1).astype(BF16)
-
-
-def product(left, right):
-    return jnp.dot(left, right, precision=lax.Precision.HIGHEST)
 
 
 def on_device(
@@ -388,11 +419,8 @@
     yic_t = per_device(np.swapaxes(yfc, 1, 2))
     yi2_t = per_device(np.swapaxes(yf1, 1, 2))
 
-    rows = jnp.transpose(fields, (1, 0, 2, 3)).reshape(xc, cin, yc * zc)
-    pooled = fields.reshape(cin, xc // 2, 2, yc // 2, 2, zc).mean(axis=(2, 4))
-    pooled = jnp.transpose(pooled, (1, 0, 2, 3)).reshape(xc // 2, cin, width)
-    bp = left16(product(bypass_in, lift), product(bypass_in, lift_bias) + bias_in)
-    pj = left16(product(proj, lift), product(proj, lift_bias) + proj_bias)
+    rows = jnp.transpose(fields, (1, 0, 2, 3)).reshape(xc * cin, yc * zc)
+    weights2 = jnp.swapaxes(spectral_out, 3, 4)
 
     vmem = pl.BlockSpec(memory_space=pltpu.VMEM)
     anywhere = pl.BlockSpec(memory_space=pl.ANY)
@@ -402,10 +430,10 @@
             kernel, A, B, xc, 1.0 / math.sqrt(cells), 1.0 / math.sqrt(cells / 4.0), math.sqrt(cells)
         ),
         out_shape=jax.ShapeDtypeStruct((xc, cin, yc * zc), F32),
-        in_specs=[vmem] * 12 + [pl.BlockSpec(memory_space=pltpu.SMEM)] + [anywhere] * 7,
+        in_specs=[vmem] * 11 + [pl.BlockSpec(memory_space=pltpu.SMEM)] + [anywhere] * 7,
         out_specs=vmem,
         scratch_shapes=[
-            V(spectral_in.shape, F32), V(spectral_out.shape, F32),
+            V(spectral_in.shape, F32), V(weights2.shape, F32),
             V(tx_t.shape[1:], BF16), V(yf1_t.shape[1:], BF16), V(yfc_t.shape[1:], BF16),
             V(yic_t.shape[1:], BF16), V(yi2_t.shape[1:], BF16),
             V((N, cin, LB), F32), V((N, cin, LB), F32), V((LB, LB), F32),
@@ -416,6 +444,7 @@
             V((C1, LB), F32), V((B, C1, LB), F32),
             V((IL, C1, 2 * LB), F32), V((A, IL, C1, 2 * LB), F32),
             V((xc // 2, C1, width), F32), V((KX, C2, LB), F32), V((KX, C1, 2 * LB), F32),
+            V((xc // 2, 16, width), BF16), V((xc, 16, yc * zc), BF16), V((16, yc * zc), F32),
             pltpu.SemaphoreType.DMA((7,)),
             pltpu.SemaphoreType.DMA((N + 3 * B + 3 * A,)), pltpu.SemaphoreType.DMA((N + 3 * B + 3 * A,)),
         ],
@@ -423,9 +452,9 @@
             collective_id=0, has_side_effects=True, vmem_limit_bytes=60 * 1024 * 1024
         ),
     )(
-        rows.reshape(xc * cin, yc * zc), right16(pooled), right16(rows), lift, lift_bias[:, None], bp,
-        hi_lo(bypass_out), bias_out[:, None], hi_lo(proj), pj, jnp.asarray(tzf), jnp.asarray(tzi),
-        jnp.asarray(cs), spectral_in, spectral_out, tx_t, yf1_t, yfc_t, yic_t, yi2_t,
+        rows, lift.T, lift_bias[None], bypass_in.T, bias_in[None], bypass_out, bias_out[None], proj,
+        proj_bias[None], jnp.asarray(tzf), jnp.asarray(tzi),
+        jnp.asarray(cs), spectral_in, weights2, tx_t, yf1_t, yfc_t, yic_t, yi2_t,
     )
     return jnp.transpose(out.reshape(xc, cin, yc, zc), (1, 0, 2, 3))
 

time: 99 us -> 79.1 us (0.80)
  local copies, waits for them, and re-layouts: 12.5 us -> 4.19 us
  other arithmetic: 6.86 us -> 0 us
  matrix products: 3.3 us -> 0 us
  Pallas kernels: 74.9 us -> 73.8 us
    unnamed x9 -> x1, local copies, waits for them, and re-layouts: 5.68 us -> 0.96 us
    dot_general x4 -> x0, matrix products: 3.3 us -> none  [product(): return jnp.dot(left, right, precision=lax.Precision.HIGHEST)]
    another operation x6 -> x0, other arithmetic: 3.13 us -> none  [the longest x4 2.62 us: hi_lo(): return jnp.stack([high.astype(BF16), rough(value - high).astype(BF16)])]
    broadcast_in_dim x7 -> x0, local copies, waits for them, and re-layouts: 2.99 us -> none  [the longest x1 1.34 us: on_device(): lift_bias[:, None]]
    concatenate x2 -> x0, other arithmetic: 2.3 us -> none  [right16(): return jnp.concatenate([high, low, high, ones], axis=1).astype(BF16)]
    concatenate x4 -> x0, local copies, waits for them, and re-layouts: 1.49 us -> none  [the longest x3 1.42 us: left16(): jnp.concatenate([high, high, low, b0[:, None], b1[:, None], b2[:, None],...]
    reduce_sum x1 -> x0, other arithmetic: 1.42 us -> none  [on_device(): pooled = fields.reshape(cin, xc // 2, 2, yc // 2, 2, zc).mean(axis=(2, 4))]
    pallas_call x1, Pallas kernels: 74.9 us -> 73.8 us  [on_device(): pl.pallas_call(functools.partial(kernel, A, B, xc, 1.0 / math.sqrt(cells)...]
where the time goes in v2:
time: 79.1 us; the launch traced here: 78 us
  Pallas kernels  73.8 us (93%)
  local copies, waits for them, and re-layouts  4.19 us (5%)
    pallas_call x1, Pallas kernels, on_device(): pl.pallas_call(functools.partial(kernel, A, B, xc, 1.0 / math.sqrt(cells)...  73.8 us
    reshape x2, local copies, waits for them, and re-layouts, on_device(): return jnp.transpose(out.reshape(xc, cin, yc, zc), (1, 0, 2, 3))  2.15 us

profile of v2, /device:TPU:0, one launch (start us, length us, event | category | flops | bytes accessed | tf_op | source)
XLA Modules:
  0.0 78.0 jit_solution(8892683384621596545)
XLA Ops:
  0.0 1.1 %copy.20 = f32[16,4,16,128]{3,2,1,0:T(8,128)S(1)} copy(f32[16,4,16,128]{3,2,0,1:T(8,128)} %bitcast.19) | data formatting | bytes 1048576 | tf_op jit(solution)/shard_map/transpose | solution.py:422
  1.1 1.0 %copy.25 = f32[8,8,16,128]{3,1,2,0:T(8,128)} copy(f32[8,8,16,128]{3,2,1,0:T(8,128)S(1)} %bitcast.16) | data formatting | bytes 1048576
  2.0 73.8 %shard_map.181 = f32[16,4,2048]{2,1,0:T(4,128)} custom-call(f32[64,2048]{1,0:T(8,128)} %bitcast.18, f32[4,32]{1,0:T(4,128)} %bitcast.21, f32[1,32]{1,0:T(1,128)} %bitcast.22, f32[32,64]{1,0:T(8,128)} %bitcast.20, f32[1,64]{1,0:T(1,128)} %bitcast.23, f32[32,64]{1,0:T(8,128)} %wo_ref.1, f32[1,32]{1,0:T(1,128)} %bitcast.24, f32[4,32]{1,0:T(4,128)} %pr_ref.1, ...), custom_call_target="tpu_custom_call" | custom-call | tf_op jit(solution)/shard_map/pallas_call | solution.py:428
  75.9 1.3 %reshape.7 = f32[16,4,16,128]{3,2,1,0:T(8,128)S(1)} reshape(f32[16,4,2048]{2,1,0:T(4,128)} %shard_map.181) | data formatting | bytes 1048576 | tf_op jit(solution)/shard_map/reshape | solution.py:459
  77.2 0.8 %copy.26 = f32[16,4,16,128]{3,2,0,1:T(8,128)} copy(f32[16,4,16,128]{3,2,1,0:T(8,128)S(1)} %reshape.7) | data formatting | bytes 1048576 | tf_op jit(solution)/shard_map/reshape | solution.py:459

commit v3 on v2

--- a/solution.py
+++ b/solution.py
@@ -14,6 +14,7 @@
 KZ = 8
 YB = 8
 LB = 128
+GROUP = 4
 F32 = jnp.float32
 BF16 = jnp.bfloat16
 MESH = pl.DeviceIdType.MESH
@@ -28,6 +29,11 @@
     high = table.astype(np.float32).astype(jnp.bfloat16)
     low = (table - high.astype(np.float64)).astype(np.float32).astype(jnp.bfloat16)
     return np.stack([high, low])
+
+
+def stacked(table):
+    high, low = halves(table)
+    return np.concatenate([high, high, low], axis=0)
 
 
 def angles(places, frequency, length):
@@ -77,6 +83,18 @@
     return jnp.dot(a, b, preferred_element_type=F32)
 
 
+def tall(a):
+    return jnp.concatenate([a[0], a[1], a[0]], axis=1)
+
+
+def deep(a):
+    return jnp.concatenate([a[0], a[1], a[0]], axis=0)
+
+
+def wide(a):
+    return jnp.concatenate([a[0], a[0], a[1]], axis=1)
+
+
 def mul3(a, b):
     return mul(a[0], b[0]) + (mul(a[1], b[0]) + mul(a[0], b[1]))
 
@@ -91,7 +109,7 @@
     tzf_ref, tzi_ref, cs_ref, w1_hbm, w2_hbm, tx_hbm, yf1_hbm, yfc_hbm, yic_hbm, yi2_hbm,
     o_ref,
     w1, w2, tx, yf1, yfc, yic, yi2,
-    buf1, r1, mx, mt1, ag1, yb1, ya1, zc, fx2, r2, buf2, r3, mt2, ag2, yb2, ya2, nar, yr1, yr2, pk_ref, fk_ref, t16,
+    buf1, r1, mx, mt1, ag1, yb1, ya1, zc, fx2, r2, buf2, r3, mt2, ag2, yb2, ya2, nar, yr1, yr2, pk_ref, fk_ref, t16, bd,
     csem, ssem, rsem,
 ):
     a = lax.axis_index("gx")
@@ -133,11 +151,10 @@
     def rot_i(v):
         return pltpu.roll(v, LB // 2, 1) * -sign_f
 
-    tzf = (tzf_ref[0], tzf_ref[1])
-    width = tzf_ref.shape[1]
+    width = tzi_ref.shape[1]
     zs = []
     for ch in range(2):
-        zs.append(mul3(split(f_ref[:, ch * width:(ch + 1) * width]), tzf))
+        zs.append(mul(tall(split(f_ref[:, ch * width:(ch + 1) * width])), tzf_ref[...]))
     loads[0].wait()
     us = []
     for z in zs:
@@ -192,9 +209,19 @@
         lift8, pr_ref[...], (((1,), (1,)), ((), ())), precision=highest, preferred_element_type=F32
     )
     pl16 = left16(m, m[CIN:CIN + 1] + pb_ref[...])
-    wo2 = split(wo_ref[...])
-    pr2 = split(pr_ref[...])
     t16[...] = jnp.ones_like(t16)
+
+    def diagonal(value):
+        rows, cols = value.shape
+        bd[...] = jnp.zeros_like(bd)
+        for g in range(GROUP):
+            bd[g * rows:(g + 1) * rows, g * cols:(g + 1) * cols] = value
+        return bd[0:GROUP * rows, 0:GROUP * cols]
+
+    bp_bd = diagonal(bp16.astype(F32)).astype(BF16)
+    pl_bd = diagonal(pl16.astype(F32)).astype(BF16)
+    wo_bd = wide(split(diagonal(wo_ref[...])))
+    pr_bd = wide(split(diagonal(pr_ref[...])))
     for step in range(1, N):
         peer = lax.rem(me + step, N)
         pltpu.make_async_remote_copy(
@@ -202,29 +229,51 @@
             device_id=(peer // B, lax.rem(peer, B)), device_id_type=MESH,
         ).wait_recv()
 
-    first_slot = {1: N, 2: N + B, 3: N + B + A, 4: N + B + 2 * A, 5: N + 2 * B + 2 * A, 6: N + 3 * B + 2 * A}
-
-    def spread(source, target, axis, count, mine, slot):
-        copies = []
-        arrivals = []
-        base = first_slot[slot]
-        for step in range(1, count):
-            peer = lax.rem(mine + step, count)
-            where = (peer, b) if axis == "gx" else (a, peer)
-            for index, group in ((mine, copies), (peer, arrivals)):
-                group.append(pltpu.make_async_remote_copy(
-                    src_ref=source(peer), dst_ref=target.at[index],
-                    send_sem=ssem.at[base + peer], recv_sem=rsem.at[base + index],
-                    device_id=where, device_id_type=MESH,
-                ))
-        for copy in copies:
-            copy.start()
-        sends.extend(copies)
-        return arrivals
-
-    def arrive(copies):
-        for copy in copies:
-            copy.wait_recv()
+    own = b // H
+    gy_slot = [N, N + B, N + 2 * B]
+    gx_slot = [N + 3 * B, N + 3 * B + KX, N + 3 * B + 2 * KX]
+
+    def to_gy(source, target, slot, peer, index):
+        return pltpu.make_async_remote_copy(
+            src_ref=source, dst_ref=target.at[index], send_sem=ssem.at[gy_slot[slot] + peer],
+            recv_sem=rsem.at[gy_slot[slot] + index], device_id=(a, peer), device_id_type=MESH,
+        )
+
+    def to_gx(source, target, slot, peer, index, il):
+        return pltpu.make_async_remote_copy(
+            src_ref=source, dst_ref=target.at[index, il],
+            send_sem=ssem.at[gx_slot[slot] + peer * IL + il],
+            recv_sem=rsem.at[gx_slot[slot] + index * IL + il],
+            device_id=(peer, b), device_id_type=MESH,
+        )
+
+    def send(copy):
+        copy.start()
+        sends.append(copy)
+
+    def gather(block, ag, slot):
+        for step in range(1, B):
+            peer = lax.rem(b + step, B)
+            send(to_gy(block, ag, slot, peer, b))
+
+    def expand(block, ag, table, yb, ya, slot, gx):
+        for s in range(IL):
+            il = lax.rem(own + s, IL)
+            for t in range(1 if s == 0 else 0, H):
+                source = il * H + lax.rem(b + t, H)
+                to_gy(block, ag, slot, source, source).wait_recv()
+            rows = jnp.concatenate([ag[il * H + h] for h in range(H)], axis=1)
+            y = mul3(split(rows), (table[0], table[1]))
+            yb[il] = y
+            ya[a, il] = y
+            for step in range(1, A):
+                peer = lax.rem(a + step, A)
+                send(to_gx(yb.at[il], ya, gx, peer, a, il))
+        for s in range(IL):
+            il = lax.rem(own + s, IL)
+            for step in range(1, A):
+                peer = lax.rem(a + step, A)
+                to_gx(yb.at[il], ya, gx, peer, peer, il).wait_recv()
 
     def mix(st, w, width_out):
         mx[...] = jnp.zeros_like(mx)
@@ -249,7 +298,7 @@
     mixed = mix(st, w1, C2)
     mt1[...] = mixed
     ag1[b] = mixed
-    copies = spread(lambda peer: mt1, ag1, "gy", B, b, 1)
+    gather(mt1, ag1, 0)
     zn = width // YB
 
     def fill(value):
@@ -272,58 +321,69 @@
         ]
         pk_ref[x] = fill(jnp.concatenate(pieces, axis=1) * 0.25)
     loads[3].wait()
-    arrive(copies)
-
-    def y_back(ag, table):
-        rows = [jnp.concatenate([ag[i * H + h] for i in range(IL)], axis=0) for h in range(H)]
-        return mul3(split(jnp.concatenate(rows, axis=1)), (table[0], table[1]))
-
-    y = y_back(ag1, yic).reshape(IL, C2, LB)
-    yb1[...] = y
-    ya1[a] = y
-    arrive(spread(lambda peer: yb1, ya1, "gx", A, a, 2))
+    expand(mt1, ag1, yic, yb1, ya1, 0, 0)
     for i in range(KX):
         yr1[i] = rot_i(ya1[i // IL, i % IL])
 
     HC = hx * KX
 
-    def coarse_step(x, carry):
-        acc = jnp.zeros((C2, LB), F32)
-        for i in range(KX):
-            c = cs_ref[a, x * KX + i]
-            s = cs_ref[a, HC + x * KX + i]
-            acc = acc + (c * ya1[i // IL, i % IL] + s * yr1[i])
-        v = mul3(split(acc), (tzi_ref[0], tzi_ref[1])) + mul(bp16, pk_ref[x])
-        g = split(gelu(v))
-        nar[x] = mul3(wo2, g)
-        zc[x] = mul3(g, (tzf_ref[0], tzf_ref[1]))
+    def coarse_step(group, carry):
+        parts = []
+        for xx in range(GROUP):
+            x = group * GROUP + xx
+            acc = jnp.zeros((C2, LB), F32)
+            for i in range(KX):
+                c = cs_ref[a, x * KX + i]
+                s = cs_ref[a, HC + x * KX + i]
+                acc = acc + (c * ya1[i // IL, i % IL] + s * yr1[i])
+            parts.append(acc)
+        v = mul(tall(split(jnp.concatenate(parts, axis=0))), tzi_ref[...])
+        near = jnp.concatenate([pk_ref[group * GROUP + xx] for xx in range(GROUP)], axis=0)
+        g = split(gelu(v + mul(bp_bd, near)))
+        narrow = mul(wo_bd, deep(g))
+        wave = mul(tall(g), tzf_ref[...])
+        for xx in range(GROUP):
+            nar[group * GROUP + xx] = narrow[xx * C1:(xx + 1) * C1]
+            zc[group * GROUP + xx] = wave[xx * C2:(xx + 1) * C2]
         return carry
 
-    lax.fori_loop(0, hx, coarse_step, 0)
-
-    def x_step(i, carry):
-        re = jnp.zeros((C2, LB), F32)
-        im = jnp.zeros((C2, LB), F32)
-        for x in range(hx):
-            re = re + cs_ref[a, x * KX + i] * zc[x]
-            im = im + cs_ref[a, HC + x * KX + i] * zc[x]
-        fx2[i // IL, i % IL] = re + rot_f(im)
-        return carry
-
-    lax.fori_loop(0, KX, x_step, 0)
-    copies = spread(lambda peer: fx2.at[peer], r2, "gx", A, a, 3)
-    r2[a] = fx2[a]
+    lax.fori_loop(0, hx // GROUP, coarse_step, 0)
+
+    order = [lax.rem(own + 1 + s, IL) for s in range(IL)]
+    for il in order:
+        for t in range(A):
+            peer = lax.rem(a + 1 + t, A)
+            i = peer * IL + il
+            re = jnp.zeros((C2, LB), F32)
+            im = jnp.zeros((C2, LB), F32)
+            for x in range(hx):
+                re = re + cs_ref[a, x * KX + i] * zc[x]
+                im = im + cs_ref[a, HC + x * KX + i] * zc[x]
+            value = re + rot_f(im)
+            if t < A - 1:
+                fx2[peer, il] = value
+                send(to_gx(fx2.at[peer, il], r2, 1, peer, a, il))
+            else:
+                r2[a, il] = value
     loads[4].wait()
-    arrive(copies)
-    total = jnp.sum(r2[...], axis=0).reshape(IL * C2, LB)
-    out = mul3(split(total), (yfc[0], yfc[1]))
-    for i in range(IL):
+    for s, il in enumerate(order):
+        for step in range(1, A):
+            peer = lax.rem(a + step, A)
+            to_gx(fx2.at[peer, il], r2, 1, peer, peer, il).wait_recv()
+        total = r2[0, il]
+        for peer in range(1, A):
+            total = total + r2[peer, il]
+        out = mul3(split(total), (yfc[0], yfc[1]))
         for h in range(H):
-            buf2[i * H + h] = out[i * C2:(i + 1) * C2, h * LB:(h + 1) * LB]
-    copies = spread(lambda peer: buf2.at[peer], r3, "gy", B, b, 4)
+            buf2[il * H + h] = out[:, h * LB:(h + 1) * LB]
+        for t in range(1 if s == IL - 1 else 0, H):
+            peer = il * H + lax.rem(b + t, H)
+            send(to_gy(buf2.at[peer], r3, 1, peer, b))
     r3[b] = buf2[b]
     loads[5].wait()
-    arrive(copies)
+    for step in range(1, B):
+        peer = lax.rem(b + step, B)
+        to_gy(buf2.at[peer], r3, 1, peer, peer).wait_recv()
     st = (jnp.sum(r3[...], axis=0) * scale2).T
     mixed = jnp.zeros((C1, LB), F32)
     for j in range(J):
@@ -339,13 +399,9 @@
             mixed = jnp.where(lane == q, real, jnp.where(lane == p, imag, mixed))
     mt2[...] = mixed
     ag2[b] = mixed
-    copies = spread(lambda peer: mt2, ag2, "gy", B, b, 5)
+    gather(mt2, ag2, 2)
     loads[6].wait()
-    arrive(copies)
-    y = y_back(ag2, yi2).reshape(IL, C1, 2 * LB)
-    yb2[...] = y
-    ya2[a] = y
-    arrive(spread(lambda peer: yb2, ya2, "gx", A, a, 6))
+    expand(mt2, ag2, yi2, yb2, ya2, 2, 2)
     for i in range(KX):
         for ch in range(2):
             part = slice(ch * LB, (ch + 1) * LB)
@@ -353,25 +409,36 @@
 
     FC = cells_x * KX
 
-    def fine_step(x, carry):
-        acc = jnp.zeros((C1, 2 * LB), F32)
-        for i in range(KX):
-            c = cs_ref[a, 2 * HC + x * KX + i]
-            s = cs_ref[a, 2 * HC + FC + x * KX + i]
-            acc = acc + (c * ya2[i // IL, i % IL] + s * yr2[i])
+    def fine_step(group, carry):
+        parts = []
+        for xx in range(GROUP):
+            x = group * GROUP + xx
+            acc = jnp.zeros((C1, 2 * LB), F32)
+            for i in range(KX):
+                c = cs_ref[a, 2 * HC + x * KX + i]
+                s = cs_ref[a, 2 * HC + FC + x * KX + i]
+                acc = acc + (c * ya2[i // IL, i % IL] + s * yr2[i])
+            parts.append(acc)
+        near = jnp.concatenate([fk_ref[group * GROUP + xx] for xx in range(GROUP)], axis=0)
         for ch in range(2):
-            v = mul3(split(acc[:, ch * LB:(ch + 1) * LB]), (tzi_ref[0], tzi_ref[1]))
-            pieces = []
-            for yy in range(YB):
-                at = (ch * YB + yy) // 2 * zn
-                pieces.append(nar[x // 2, :, at:at + zn])
-            v = v + jnp.concatenate(pieces, axis=1) + bo_col
-            g = split(gelu(v))
+            lines = jnp.concatenate([part[:, ch * LB:(ch + 1) * LB] for part in parts], axis=0)
+            v = mul(tall(split(lines)), tzi_ref[...])
+            rows = []
+            for xx in range(0, GROUP, 2):
+                half = nar.at[group * (GROUP // 2) + xx // 2]
+                pieces = []
+                for yy in range(YB):
+                    at = (ch * YB + yy) // 2 * zn
+                    pieces.append(half[:, at:at + zn])
+                rows += [jnp.concatenate(pieces, axis=1) + bo_col] * 2
+            g = split(gelu(v + jnp.concatenate(rows, axis=0)))
             cols = slice(ch * width, (ch + 1) * width)
-            o_ref[x, :, cols] = mul3(pr2, g) + mul(pl16, fk_ref[x, :, cols])
+            res = mul(pr_bd, deep(g)) + mul(pl_bd, near[:, cols])
+            for xx in range(GROUP):
+                o_ref[group * GROUP + xx, :, cols] = res[xx * CIN:(xx + 1) * CIN]
         return carry
 
-    lax.fori_loop(0, cells_x, fine_step, 0)
+    lax.fori_loop(0, cells_x // GROUP, fine_step, 0)
     for copy in sends:
         copy.wait_send()
 
@@ -394,8 +461,8 @@
     back = math.sqrt(2.0 / (KX * KY * KZ))
 
     tz = z_table(zc)
-    tzf = halves(tz)
-    tzi = halves(np.ascontiguousarray(tz.T) * back)
+    tzf = stacked(tz)
+    tzi = stacked(np.ascontiguousarray(tz.T) * back)
     fine_x = x_angles(A, xc, NX)
     half_x = x_angles(A, xc // 2, NX // 2)
     eye = np.eye(cin)
@@ -444,9 +511,9 @@
             V((C1, LB), F32), V((B, C1, LB), F32),
             V((IL, C1, 2 * LB), F32), V((A, IL, C1, 2 * LB), F32),
             V((xc // 2, C1, width), F32), V((KX, C2, LB), F32), V((KX, C1, 2 * LB), F32),
-            V((xc // 2, 16, width), BF16), V((xc, 16, yc * zc), BF16), V((16, yc * zc), F32),
+            V((xc // 2, 16, width), BF16), V((xc, 16, yc * zc), BF16), V((16, yc * zc), F32), V((GROUP * C2, GROUP * C2), F32),
             pltpu.SemaphoreType.DMA((7,)),
-            pltpu.SemaphoreType.DMA((N + 3 * B + 3 * A,)), pltpu.SemaphoreType.DMA((N + 3 * B + 3 * A,)),
+            pltpu.SemaphoreType.DMA((N + 3 * B + 3 * KX,)), pltpu.SemaphoreType.DMA((N + 3 * B + 3 * KX,)),
         ],
         compiler_params=pltpu.CompilerParams(
             collective_id=0, has_side_effects=True, vmem_limit_bytes=60 * 1024 * 1024

time: 79.1 us -> 64.9 us (0.82); the launches traced: 78 us -> 64.7 us
  Pallas kernels: 73.8 us -> 60.5 us
    pallas_call x1, Pallas kernels: 73.8 us -> 60.5 us  [on_device(): pl.pallas_call(functools.partial(kernel, A, B, xc, 1.0 / math.sqrt(cells)...]
where the time goes in v3:
time: 64.9 us; the launch traced here: 64.7 us
  Pallas kernels  60.5 us (93%)
  local copies, waits for them, and re-layouts  4.19 us (6%)
    pallas_call x1, Pallas kernels, on_device(): pl.pallas_call(functools.partial(kernel, A, B, xc, 1.0 / math.sqrt(cells)...  60.5 us
    reshape x2, local copies, waits for them, and re-layouts, on_device(): return jnp.transpose(out.reshape(xc, cin, yc, zc), (1, 0, 2, 3))  2.15 us

profile of v3, /device:TPU:0, one launch (start us, length us, event | category | flops | bytes accessed | tf_op | source)
XLA Modules:
  0.0 64.7 jit_solution(10444165220545485459)
XLA Ops:
  0.0 1.1 %copy.20 = f32[16,4,16,128]{3,2,1,0:T(8,128)S(1)} copy(f32[16,4,16,128]{3,2,0,1:T(8,128)} %bitcast.19) | data formatting | bytes 1048576 | tf_op jit(solution)/shard_map/transpose | solution.py:489
  1.1 1.0 %copy.25 = f32[8,8,16,128]{3,1,2,0:T(8,128)} copy(f32[8,8,16,128]{3,2,1,0:T(8,128)S(1)} %bitcast.17) | data formatting | bytes 1048576
  2.0 60.5 %shard_map.181 = f32[16,4,2048]{2,1,0:T(4,128)} custom-call(f32[64,2048]{1,0:T(8,128)} %bitcast.16, f32[4,32]{1,0:T(4,128)} %bitcast.21, f32[1,32]{1,0:T(1,128)} %bitcast.22, f32[32,64]{1,0:T(8,128)} %bitcast.20, f32[1,64]{1,0:T(1,128)} %bitcast.23, f32[32,64]{1,0:T(8,128)} %wo_ref.1, f32[1,32]{1,0:T(1,128)} %bitcast.24, f32[4,32]{1,0:T(4,128)} %pr_ref.1, ...), custom_call_target="tpu_custom_call" | custom-call | tf_op jit(solution)/shard_map/pallas_call | solution.py:495
  62.5 1.3 %reshape.7 = f32[16,4,16,128]{3,2,1,0:T(8,128)S(1)} reshape(f32[16,4,2048]{2,1,0:T(4,128)} %shard_map.181) | data formatting | bytes 1048576 | tf_op jit(solution)/shard_map/reshape | solution.py:526
  63.8 0.8 %copy.26 = f32[16,4,16,128]{3,2,0,1:T(8,128)} copy(f32[16,4,16,128]{3,2,1,0:T(8,128)S(1)} %reshape.7) | data formatting | bytes 1048576 | tf_op jit(solution)/shard_map/reshape | solution.py:526

commit v4 on v3

--- a/solution.py
+++ b/solution.py
@@ -251,28 +251,80 @@
         copy.start()
         sends.append(copy)
 
+    Q = B // 4 if B % 4 == 0 and H % (B // 4) == 0 else 1
+    R = H // Q
+    plane = b // Q
+    column = lax.rem(b, Q)
+    core = lax.rem(a, 2)
+    partner = a + 1 - 2 * core
+
     def gather(block, ag, slot):
-        for step in range(1, B):
-            peer = lax.rem(b + step, B)
-            send(to_gy(block, ag, slot, peer, b))
+        for step in range(1, B // Q):
+            send(to_gy(block, ag, slot, lax.rem(plane + step, B // Q) * Q + column, b))
+        for step in range(1, Q):
+            send(to_gy(block, ag, slot, plane * Q + lax.rem(column + step, Q), b))
 
     def expand(block, ag, table, yb, ya, slot, gx):
-        for s in range(IL):
+        def planes(s):
             il = lax.rem(own + s, IL)
-            for t in range(1 if s == 0 else 0, H):
-                source = il * H + lax.rem(b + t, H)
+            return il, [il * R + lax.rem(plane + r, R) for r in range(R)]
+
+        def relay(s):
+            for r, place in enumerate(planes(s)[1]):
+                if s == 0 and r == 0:
+                    continue
+                source = place * Q + column
                 to_gy(block, ag, slot, source, source).wait_recv()
+                for step in range(1, Q):
+                    other = lax.rem(column + step, Q)
+                    copy = pltpu.make_async_remote_copy(
+                        src_ref=ag.at[source], dst_ref=ag.at[source],
+                        send_sem=ssem.at[gy_slot[slot] + place * Q + other],
+                        recv_sem=rsem.at[gy_slot[slot] + source],
+                        device_id=(a, plane * Q + other), device_id_type=MESH,
+                    )
+                    send(copy)
+
+        def process(s):
+            il, places = planes(s)
+            for place in places:
+                for step in range(1, Q):
+                    source = place * Q + lax.rem(column + step, Q)
+                    to_gy(block, ag, slot, source, source).wait_recv()
             rows = jnp.concatenate([ag[il * H + h] for h in range(H)], axis=1)
             y = mul3(split(rows), (table[0], table[1]))
             yb[il] = y
             ya[a, il] = y
-            for step in range(1, A):
-                peer = lax.rem(a + step, A)
-                send(to_gx(yb.at[il], ya, gx, peer, a, il))
+            for step in range(1, A // 2):
+                send(to_gx(yb.at[il], ya, gx, lax.rem(a + 2 * step, A), a, il))
+            send(to_gx(yb.at[il], ya, gx, partner, a, il))
+
+        def across(s):
+            il = lax.rem(own + s, IL)
+            for step in range(1, A // 2):
+                peer = lax.rem(a + 2 * step, A)
+                to_gx(yb.at[il], ya, gx, peer, peer, il).wait_recv()
+                twin = peer + 1 - 2 * core
+                copy = pltpu.make_async_remote_copy(
+                    src_ref=ya.at[peer, il], dst_ref=ya.at[peer, il],
+                    send_sem=ssem.at[gx_slot[gx] + twin * IL + il],
+                    recv_sem=rsem.at[gx_slot[gx] + peer * IL + il],
+                    device_id=(partner, b), device_id_type=MESH,
+                )
+                send(copy)
+
+        relay(0)
+        for s in range(IL):
+            if s + 1 < IL:
+                relay(s + 1)
+            process(s)
+            if s >= 1:
+                across(s - 1)
+        across(IL - 1)
         for s in range(IL):
             il = lax.rem(own + s, IL)
-            for step in range(1, A):
-                peer = lax.rem(a + step, A)
+            for step in range(0, A // 2):
+                peer = lax.rem(partner + 2 * step, A)
                 to_gx(yb.at[il], ya, gx, peer, peer, il).wait_recv()
 
     def mix(st, w, width_out):

time: 64.9 us -> 70.3 us (1.083); the launches traced: 64.7 us -> 69.4 us
  Pallas kernels: 60.5 us -> 65.2 us
    pallas_call x1, Pallas kernels: 60.5 us -> 65.2 us  [on_device(): pl.pallas_call(functools.partial(kernel, A, B, xc, 1.0 / math.sqrt(cells)...]
where the time goes in v4:
time: 70.3 us; the launch traced here: 69.4 us
  Pallas kernels  65.2 us (93%)
  local copies, waits for them, and re-layouts  4.19 us (6%)
    pallas_call x1, Pallas kernels, on_device(): pl.pallas_call(functools.partial(kernel, A, B, xc, 1.0 / math.sqrt(cells)...  65.2 us
    reshape x2, local copies, waits for them, and re-layouts, on_device(): return jnp.transpose(out.reshape(xc, cin, yc, zc), (1, 0, 2, 3))  2.15 us

profile of v4, /device:TPU:0, one launch (start us, length us, event | category | flops | bytes accessed | tf_op | source)
XLA Modules:
  0.0 69.4 jit_solution(7124783432574131135)
XLA Ops:
  0.0 1.1 %copy.20 = f32[16,4,16,128]{3,2,1,0:T(8,128)S(1)} copy(f32[16,4,16,128]{3,2,0,1:T(8,128)} %bitcast.19) | data formatting | bytes 1048576 | tf_op jit(solution)/shard_map/transpose | solution.py:541
  1.1 1.0 %copy.25 = f32[8,8,16,128]{3,1,2,0:T(8,128)} copy(f32[8,8,16,128]{3,2,1,0:T(8,128)S(1)} %bitcast.17) | data formatting | bytes 1048576
  2.0 65.2 %shard_map.181 = f32[16,4,2048]{2,1,0:T(4,128)} custom-call(f32[64,2048]{1,0:T(8,128)} %bitcast.16, f32[4,32]{1,0:T(4,128)} %bitcast.21, f32[1,32]{1,0:T(1,128)} %bitcast.22, f32[32,64]{1,0:T(8,128)} %bitcast.20, f32[1,64]{1,0:T(1,128)} %bitcast.23, f32[32,64]{1,0:T(8,128)} %wo_ref.1, f32[1,32]{1,0:T(1,128)} %bitcast.24, f32[4,32]{1,0:T(4,128)} %pr_ref.1, ...), custom_call_target="tpu_custom_call" | custom-call | tf_op jit(solution)/shard_map/pallas_call | solution.py:547
  67.2 1.3 %reshape.7 = f32[16,4,16,128]{3,2,1,0:T(8,128)S(1)} reshape(f32[16,4,2048]{2,1,0:T(4,128)} %shard_map.181) | data formatting | bytes 1048576 | tf_op jit(solution)/shard_map/reshape | solution.py:578
  68.5 0.8 %copy.26 = f32[16,4,16,128]{3,2,0,1:T(8,128)} copy(f32[16,4,16,128]{3,2,1,0:T(8,128)S(1)} %reshape.7) | data formatting | bytes 1048576 | tf_op jit(solution)/shard_map/reshape | solution.py:578

commit v5 on v3

--- a/solution.py
+++ b/solution.py
@@ -106,9 +106,9 @@
 def kernel(
     A, B, cells_x, scale1, scale2, gain,
     f_ref, lift_ref, lbias_ref, byp_ref, bi_ref, wo_ref, bo_ref, pr_ref, pb_ref,
-    tzf_ref, tzi_ref, cs_ref, w1_hbm, w2_hbm, tx_hbm, yf1_hbm, yfc_hbm, yic_hbm, yi2_hbm,
+    tzf_ref, cs_ref, tzi_hbm, w1_hbm, w2_hbm, tx_hbm, yf1_hbm, yfc_hbm, yic_hbm, yi2_hbm,
     o_ref,
-    w1, w2, tx, yf1, yfc, yic, yi2,
+    tzi_ref, w1, w2, tx, yf1, yfc, yic, yi2,
     buf1, r1, mx, mt1, ag1, yb1, ya1, zc, fx2, r2, buf2, r3, mt2, ag2, yb2, ya2, nar, yr1, yr2, pk_ref, fk_ref, t16, bd,
     csem, ssem, rsem,
 ):
@@ -131,6 +131,7 @@
         pltpu.make_async_copy(yfc_hbm.at[b], yfc, csem.at[4]),
         pltpu.make_async_copy(w2_hbm, w2, csem.at[5]),
         pltpu.make_async_copy(yi2_hbm.at[b], yi2, csem.at[6]),
+        pltpu.make_async_copy(tzi_hbm, tzi_ref, csem.at[7]),
     ]
     for load in loads:
         load.start()
@@ -347,6 +348,7 @@
             zc[group * GROUP + xx] = wave[xx * C2:(xx + 1) * C2]
         return carry
 
+    loads[7].wait()
     lax.fori_loop(0, hx // GROUP, coarse_step, 0)
 
     order = [lax.rem(own + 1 + s, IL) for s in range(IL)]
@@ -497,10 +499,10 @@
             kernel, A, B, xc, 1.0 / math.sqrt(cells), 1.0 / math.sqrt(cells / 4.0), math.sqrt(cells)
         ),
         out_shape=jax.ShapeDtypeStruct((xc, cin, yc * zc), F32),
-        in_specs=[vmem] * 11 + [pl.BlockSpec(memory_space=pltpu.SMEM)] + [anywhere] * 7,
+        in_specs=[vmem] * 10 + [pl.BlockSpec(memory_space=pltpu.SMEM)] + [anywhere] * 8,
         out_specs=vmem,
         scratch_shapes=[
-            V(spectral_in.shape, F32), V(weights2.shape, F32),
+            V(tzi.shape, BF16), V(spectral_in.shape, F32), V(weights2.shape, F32),
             V(tx_t.shape[1:], BF16), V(yf1_t.shape[1:], BF16), V(yfc_t.shape[1:], BF16),
             V(yic_t.shape[1:], BF16), V(yi2_t.shape[1:], BF16),
             V((N, cin, LB), F32), V((N, cin, LB), F32), V((LB, LB), F32),
@@ -512,7 +514,7 @@
             V((IL, C1, 2 * LB), F32), V((A, IL, C1, 2 * LB), F32),
             V((xc // 2, C1, width), F32), V((KX, C2, LB), F32), V((KX, C1, 2 * LB), F32),
             V((xc // 2, 16, width), BF16), V((xc, 16, yc * zc), BF16), V((16, yc * zc), F32), V((GROUP * C2, GROUP * C2), F32),
-            pltpu.SemaphoreType.DMA((7,)),
+            pltpu.SemaphoreType.DMA((8,)),
             pltpu.SemaphoreType.DMA((N + 3 * B + 3 * KX,)), pltpu.SemaphoreType.DMA((N + 3 * B + 3 * KX,)),
         ],
         compiler_params=pltpu.CompilerParams(
@@ -520,8 +522,8 @@
         ),
     )(
         rows, lift.T, lift_bias[None], bypass_in.T, bias_in[None], bypass_out, bias_out[None], proj,
-        proj_bias[None], jnp.asarray(tzf), jnp.asarray(tzi),
-        jnp.asarray(cs), spectral_in, weights2, tx_t, yf1_t, yfc_t, yic_t, yi2_t,
+        proj_bias[None], jnp.asarray(tzf), jnp.asarray(cs),
+        jnp.asarray(tzi), spectral_in, weights2, tx_t, yf1_t, yfc_t, yic_t, yi2_t,
     )
     return jnp.transpose(out.reshape(xc, cin, yc, zc), (1, 0, 2, 3))
 

time: 64.9 us -> 64.7 us (level)
  no operation moved by 1% of the time
where the time goes in v5:
time: 64.7 us; the launch traced here: 64.5 us
  Pallas kernels  60.3 us (93%)
  local copies, waits for them, and re-layouts  4.19 us (6%)
    pallas_call x1, Pallas kernels, on_device(): pl.pallas_call(functools.partial(kernel, A, B, xc, 1.0 / math.sqrt(cells)...  60.3 us
    reshape x2, local copies, waits for them, and re-layouts, on_device(): return jnp.transpose(out.reshape(xc, cin, yc, zc), (1, 0, 2, 3))  2.15 us

profile of v5, /device:TPU:0, one launch (start us, length us, event | category | flops | bytes accessed | tf_op | source)
XLA Modules:
  0.0 64.5 jit_solution(11612581790981627121)
XLA Ops:
  0.0 1.1 %copy.20 = f32[16,4,16,128]{3,2,1,0:T(8,128)S(1)} copy(f32[16,4,16,128]{3,2,0,1:T(8,128)} %bitcast.19) | data formatting | bytes 1048576 | tf_op jit(solution)/shard_map/transpose | solution.py:491
  1.1 1.0 %copy.25 = f32[8,8,16,128]{3,1,2,0:T(8,128)} copy(f32[8,8,16,128]{3,2,1,0:T(8,128)S(1)} %bitcast.17) | data formatting | bytes 1048576
  2.0 60.3 %shard_map.181 = f32[16,4,2048]{2,1,0:T(4,128)} custom-call(f32[64,2048]{1,0:T(8,128)} %bitcast.16, f32[4,32]{1,0:T(4,128)} %bitcast.21, f32[1,32]{1,0:T(1,128)} %bitcast.22, f32[32,64]{1,0:T(8,128)} %bitcast.20, f32[1,64]{1,0:T(1,128)} %bitcast.23, f32[32,64]{1,0:T(8,128)} %wo_ref.1, f32[1,32]{1,0:T(1,128)} %bitcast.24, f32[4,32]{1,0:T(4,128)} %pr_ref.1, ...), custom_call_target="tpu_custom_call" | custom-call | tf_op jit(solution)/shard_map/pallas_call | solution.py:497
  62.3 1.3 %reshape.7 = f32[16,4,16,128]{3,2,1,0:T(8,128)S(1)} reshape(f32[16,4,2048]{2,1,0:T(4,128)} %shard_map.181) | data formatting | bytes 1048576 | tf_op jit(solution)/shard_map/reshape | solution.py:528
  63.6 0.8 %copy.26 = f32[16,4,16,128]{3,2,0,1:T(8,128)} copy(f32[16,4,16,128]{3,2,1,0:T(8,128)S(1)} %reshape.7) | data formatting | bytes 1048576 | tf_op jit(solution)/shard_map/reshape | solution.py:528
